TPU v7x, 256 devices: a whole 4x4x8 slice. The times are simulated.
256 devices in a mesh: ctx: 128 (over z, x_lo, y, core), head: 2 (over x_hi).
Axes of the slice: x: 4 (x_hi: 2, x_lo: 2; x = x_hi * 2 + x_lo), y: 4, z: 8, core: 2. Of those that a mesh axis runs over, the one named last changes fastest.
Arguments:
- queries: bfloat16 [65536, 2048], P('ctx', 'head'), may hold values from -13 to 13, as said below
- keys: bfloat16 [65536, 512], P('ctx', 'head'), may hold values from -13 to 13
- values: bfloat16 [65536, 512], P('ctx', 'head'), may hold values from -24 to 24
- positions: int32 [65536], P('ctx'), may hold values from 0 to 32767, as said below
- out_weight: bfloat16 [2048, 4096], P(None, 'head'), may hold values from -0.125 to 0.125
Outputs:
- mixed: bfloat16 [65536, 4096], P('ctx', 'head')
Inputs may be any that keep to these rules, and one draw needn't show every extreme that they name: queries, keys: every entry lies in the stated range. positions[r] is 0 where the token at sequence position g(r) begins a document and one more than the position of the token at g(r) - 1 otherwise; documents begin at sequence positions 0 and 32768 and possibly elsewhere in the first half; the second half is one document.
All inputs are finite; a program needn't handle non-finite values.
Results may differ from a plain program's by a relative error of at most 0.012.
The roundings to bfloat16 on the way count: a program that leaves them out, or rounds other values in their place, can miss the bound.
Values may be sent and summed in bfloat16 or wider, within the bound.
A program may use at most 128 MiB of HBM per device.

v0:
```python
import math

import jax
import jax.numpy as jnp
import numpy as np
from jax import lax
from jax.sharding import PartitionSpec as P

HEAD_SIZE = 128
STEPS = 4


neg_large = -1e30


def passed_along(value, axis, steps):
    count = lax.axis_size(axis)
    pairs = [(source, (source + steps) % count) for source in range(count)]
    return lax.ppermute(value, axis, pairs)


def rotate(block, positions, width):
    halfway = width // 2
    table = np.power(500000.0, -2.0 * np.arange(halfway) / width).astype(np.float32)
    angle = positions.astype(jnp.float32)[:, None] * jnp.asarray(table, dtype=jnp.float32)[None, :]
    cosine = jnp.cos(angle)[:, None, :]
    sinus = jnp.sin(angle)[:, None, :]
    number = block.shape[0]
    groups = block.shape[1] // width
    split_up = block.astype(jnp.float32).reshape(number, groups, width)
    leading = split_up[:, :, :halfway]
    trailing = split_up[:, :, halfway:]
    turned = jnp.concatenate(
        [leading * cosine - trailing * sinus, trailing * cosine + leading * sinus], axis=2
    )
    return turned.reshape(number, groups * width).astype(jnp.bfloat16)


def make_index(block_number, cycle_size, number):
    halfway = number // 2
    within = jnp.arange(number, dtype=jnp.int32)
    early = block_number * halfway + within
    late = (2 * cycle_size - 1 - block_number) * halfway + within - halfway
    return jnp.where(within < halfway, early, late)


def attend(
    state, query_part, query_index, query_start, key_part, value_part, key_index, query_group
):
    maxima, totals, sums = state
    number = query_part.shape[0]
    shaped_query = query_part.reshape(number, -1, query_group, HEAD_SIZE)
    shaped_key = key_part.reshape(key_part.shape[0], -1, HEAD_SIZE)
    shaped_value = value_part.reshape(value_part.shape[0], -1, HEAD_SIZE)
    scores = jnp.einsum(
        "qhgd,khd->hgqk", shaped_query, shaped_key, preferred_element_type=jnp.float32
    ) * (1.0 / math.sqrt(HEAD_SIZE))
    allowed = (key_index[None, :] <= query_index[:, None]) & (
        key_index[None, :] >= query_start[:, None]
    )
    scores = jnp.where(allowed, scores, neg_large)
    updated = jnp.maximum(maxima, jnp.max(scores, axis=3))
    weights = jnp.where(allowed, jnp.exp(scores - updated[..., None]), 0.0)
    factor = jnp.exp(maxima - updated)
    totals = totals * factor + jnp.sum(weights, axis=3)
    added = jnp.einsum(
        "hgqk,khd->qhgd",
        weights.astype(jnp.bfloat16),
        shaped_value,
        preferred_element_type=jnp.float32,
    )
    sums = sums * jnp.transpose(factor, (2, 0, 1))[..., None] + added
    return (updated, totals, sums)


def attend_rows(
    state, lower, upper, q_rot, index_of, doc_start, key_part, value_part, key_index, query_group
):
    maxima, totals, sums = state
    sliced = (maxima, totals, sums)
    new_max, new_total, new_sums = attend(
        sliced, q_rot, index_of, doc_start, key_part, value_part, key_index, query_group
    )
    return (
        maxima.at[:, :, lower:upper].set(new_max),
        totals.at[:, :, lower:upper].set(new_total),
        sums.at[lower:upper].set(new_sums),
    )


def shards(queries, keys, values, positions, out_weight):
    number = queries.shape[0]
    cycle_size = lax.axis_size("ctx")
    rank = lax.axis_index("ctx")
    kv_local = keys.shape[1] // HEAD_SIZE
    query_group = queries.shape[1] // keys.shape[1]
    index_of = make_index(rank, cycle_size, number)
    doc_start = index_of - positions
    q_rot = rotate(queries, positions, HEAD_SIZE)
    rotary_keys = rotate(keys, positions, HEAD_SIZE)
    state = (
        jnp.full((kv_local, query_group, number), neg_large, jnp.float32),
        jnp.zeros((kv_local, query_group, number), jnp.float32),
        jnp.zeros((number, kv_local, query_group, HEAD_SIZE), jnp.float32),
    )
    state = attend_rows(
        state, 0, number, q_rot, index_of, doc_start, rotary_keys, values, index_of, query_group
    )
    travel = (rotary_keys, values)
    for step in range(1, STEPS):
        travel = passed_along((travel[0], travel[1]), "ctx", 1)
        key_row_slice, value_rows = travel
        source = (rank - step) % cycle_size
        key_index = make_index(source, cycle_size, number)
        state = attend_rows(
            state,
            0,
            number,
            q_rot,
            index_of,
            doc_start,
            key_row_slice,
            value_rows,
            key_index,
            query_group,
        )
    maxima, totals, sums = state
    attended = (
        (sums / jnp.transpose(totals, (2, 0, 1))[..., None])
        .reshape(number, kv_local * query_group * HEAD_SIZE)
        .astype(jnp.bfloat16)
    )
    mixed = jnp.dot(
        lax.all_gather(attended, "head", axis=1, tiled=True),
        out_weight,
        preferred_element_type=jnp.float32,
    )
    return mixed.astype(jnp.bfloat16)


def solution(mesh):
    in_specs = (P("ctx", "head"), P("ctx", "head"), P("ctx", "head"), P("ctx"), P(None, "head"))
    out_specs = P("ctx", "head")
    return jax.shard_map(shards, mesh=mesh, in_specs=in_specs, out_specs=out_specs, check_vma=False)
```

profile of v0, /device:TPU:1, one launch (start us, length us, event | category | flops | bytes accessed | tf_op | source)
XLA Modules:
  0.0 138.5 jit_solution(5916004114600088739)
XLA Ops:
  6.5 0.0 copy-start.1
  6.5 0.0 all-gather.2.cloned.1.call-start
  6.5 1.2 copy.18
  7.7 0.1 fusion.58
  7.8 0.2 copy.54
  8.0 0.2 copy.55
  8.2 0.8 fusion.40
  9.0 1.6 %multiply_cosine_fusion = (f32[512,64]{1,0:T(8,128)S(1)}, f32[512,64]{1,0:T(8,128)S(1)}) fusion(f32[64]{0:T(128)} %constant.404.clone, f32[512]{0:T(512)S(1)} %get-tuple-element.249), kind=kLoop, calls=%fused_computation.50 | loop fusion | flops 32768 | bytes 264448 | tf_op jit(solution)/shard_map/cos | solution.py:26
  10.6 0.1 multiply_subtract_fusion
  10.8 0.1 maximum_convert_fusion
  10.9 0.1 copy.25
  11.1 2.8 %collective-permute-start = (bf16[512,256]{0,1:T(8,128)(2,1)S(1)}, bf16[512,256]{0,1:T(8,128)(2,1)}, u32[]{:S(2)}, u32[]{:S(2)}) collective-permute-start(bf16[512,256]{0,1:T(8,128)(2,1)S(1)} %bitcast.211), channel_id=1, source_target_pairs={{0,2},{2,4},{4,6},{6,8},{8,10},{10,12},{12,14},{14,16},{16,18},{18... | collective-permute-start | bytes 786440 | tf_op jit(solution)/shard_map/ppermute | solution.py:19
  13.8 0.1 collective-permute-start.1
  13.9 1.1 copy.47
  15.1 0.0 copy-done.1
  15.1 0.2 convert_bitcast_fusion
  15.3 0.5 copy.58
  15.8 0.7 fusion.57
  16.5 0.8 subtract_convert_fusion
  17.3 0.6 pad_maximum_fusion
  17.9 1.0 compare_and_fusion.3
  18.9 4.7 %fusion = (f32[2,4,512]{2,1,0:T(4,128)S(1)}, f32[2,512,512,4]{2,1,3,0:T(8,128)}) fusion(pred[512,512]{0,1:T(8,128)(4,1)S(1)} %get-tuple-element.242, bf16[512,2,4,128]{3,0,2,1:T(8,128)(2,1)S(1)} %bitcast.202, bf16[512,2,128]{2,0,1:T(8,128)(2,1)S(1)} %maximum_convert_fusion), kind=kOutput, calls=%fused_computation.8 | convolution fusion | flops 543158272 | bytes 9977856 | tf_op jit(solution)/shard_map/qhgd,khd->hgqk/dot_general | solution.py:55
  23.6 0.0 collective-permute-done.1
  23.6 0.9 copy.27
  24.5 1.6 %collective-permute-start.3 = (bf16[512,256]{1,0:T(8,128)(2,1)S(1)}, bf16[512,256]{1,0:T(8,128)(2,1)S(1)}, u32[]{:S(2)}, u32[]{:S(2)}) collective-permute-start(bf16[512,256]{1,0:T(8,128)(2,1)S(1)} %collective-permute-done.1), channel_id=1, source_target_pairs={{0,2},{2,4},{4,6},{6,8},{8,10},{10,12},{12,14},{14,16},{16,18},{18... | collective-permute-start | bytes 786440 | tf_op jit(solution)/shard_map/ppermute | solution.py:19
  26.1 0.0 collective-permute-done
  26.1 0.1 collective-permute-start.2
  26.2 5.9 %fusion.1 = (f32[2,4,512]{2,1,0:T(4,128)S(1)}, f32[2,512,512,4]{2,1,3,0:T(8,128)}) fusion(pred[512,512]{0,1:T(8,128)(4,1)S(1)} %get-tuple-element.243, bf16[512,2,128,1]{0,2,3,1:T(8,128)(2,1)} %bitcast.45, bf16[512,2,4,128]{3,0,2,1:T(8,128)(2,1)S(1)} %bitcast.203), kind=kOutput, calls=%fused_computation.9 | convolution fusion | flops 543158272 | bytes 9977856 | tf_op jit(solution)/shard_map/qhgd,khd->hgqk/dot_general | solution.py:55
  32.0 0.0 collective-permute-done.3
  32.1 0.8 copy.30
  32.9 1.2 collective-permute-start.5
  34.1 0.0 collective-permute-done.2
  34.1 0.5 collective-permute-start.4
  34.7 0.0 slice-start
  34.7 2.0 %fusion.2 = (f32[2,4,512]{2,1,0:T(4,128)S(1)}, f32[2,512,512,4]{2,1,3,0:T(8,128)S(1)}) fusion(pred[512,512]{0,1:T(8,128)(4,1)S(1)} %get-tuple-element.244, bf16[512,2,128,1]{0,2,3,1:T(8,128)(2,1)S(1)} %bitcast.209, bf16[512,2,4,128]{3,0,2,1:T(8,128)(2,1)S(1)} %bitcast.204), kind=kOutput, calls=%fused_computation.10 | convolution fusion | flops 543158272 | bytes 9977856 | tf_op jit(solution)/shard_map/qhgd,khd->hgqk/dot_general | solution.py:55
  36.7 6.2 %collective-permute-done.4 = bf16[512,256]{0,1:T(8,128)(2,1)S(1)} collective-permute-done((bf16[512,256]{0,1:T(8,128)(2,1)S(1)}, bf16[512,256]{0,1:T(8,128)(2,1)S(1)}, u32[]{:S(2)}, u32[]{:S(2)}) %collective-permute-start.4) | collective-permute-done | bytes 262176 | tf_op jit(solution)/shard_map/ppermute | solution.py:19
  42.9 0.0 slice-start.1
  42.9 2.0 %fusion.3 = (f32[2,4,512]{2,1,0:T(4,128)S(1)}, f32[2,512,512,4]{2,1,3,0:T(8,128)S(1)}) fusion(pred[512,512]{0,1:T(8,128)(4,1)S(1)} %get-tuple-element.245, bf16[512,2,128,1]{0,2,3,1:T(8,128)(2,1)S(1)} %bitcast.210, bf16[512,2,4,128]{3,0,2,1:T(8,128)(2,1)S(1)} %bitcast.205), kind=kOutput, calls=%fused_computation.11 | convolution fusion | flops 543158272 | bytes 9977856 | tf_op jit(solution)/shard_map/qhgd,khd->hgqk/dot_general | solution.py:55
  44.9 0.0 copy-start
  45.0 0.0 slice-done
  45.0 0.1 slice-done.1
  45.1 2.0 %fusion.4 = f32[2,4,512]{2,1,0:T(4,128)S(1)} fusion(f32[2,512,512,4]{2,1,3,0:T(8,128)S(1)} %bitcast.199, f32[2,4,512]{2,1,0:T(4,128)S(1)} %get-tuple-element.241, pred[512,512]{0,1:T(8,128)(4,1)S(1)} %get-tuple-element.242), kind=kLoop, calls=%fused_computation.12 | loop fusion | flops 10481664 | bytes 8683520 | tf_op jit(solution)/shard_map/reduce_sum | solution.py:65
  47.1 0.0 slice-start.2
  47.1 0.0 slice-start.3
  47.1 3.8 %fusion.18 = f32[2,4,512,128]{2,3,1,0:T(8,128)} fusion(bf16[512,2,128,1]{0,2,3,1:T(8,128)(2,1)S(1)} %bitcast.212, f32[2,512,512,4]{2,1,3,0:T(8,128)S(1)} %bitcast.199, f32[2,4,512]{2,1,0:T(4,128)S(1)} %get-tuple-element.241, pred[512,512]{0,1:T(8,128)(4,1)S(1)} %get-tuple-element.242), kind=kOutput, calls=%fused_computation.23 | convolution fusion | flops 547356672 | bytes 11026432 | tf_op jit(solution)/shard_map/hgqk,khd->qhgd/dot_general | solution.py:66
  51.0 0.0 copy-start.2
  51.0 0.0 slice-done.2
  51.0 1.0 slice-done.3
  52.0 2.0 %fusion.6 = f32[2,4,512]{2,1,0:T(4,128)S(1)} fusion(f32[2,512,512,4]{2,1,3,0:T(8,128)S(1)} %bitcast.201, f32[2,4,512]{2,1,0:T(4,128)S(1)} %get-tuple-element.230, pred[512,512]{0,1:T(8,128)(4,1)S(1)} %get-tuple-element.243), kind=kLoop, calls=%fused_computation.14 | loop fusion | flops 10481664 | bytes 8683520 | tf_op jit(solution)/shard_map/reduce_sum | solution.py:65
  54.0 0.0 copy-done.2
  54.0 3.9 %fusion.16 = f32[2,4,512,128]{2,3,1,0:T(8,128)} fusion(bf16[512,2,128,1]{0,2,3,1:T(8,128)(2,1)S(1)} %bitcast.213, f32[2,512,512,4]{2,1,3,0:T(8,128)S(1)} %bitcast.201, f32[2,4,512]{2,1,0:T(4,128)S(1)} %get-tuple-element.230, pred[512,512]{0,1:T(8,128)(4,1)S(1)} %get-tuple-element.243), kind=kOutput, calls=%fused_computation.22 | convolution fusion | flops 547356672 | bytes 11026432 | tf_op jit(solution)/shard_map/hgqk,khd->qhgd/dot_general | solution.py:66
  57.9 0.0 copy-start.3
  57.9 2.0 %fusion.8 = f32[2,4,512]{2,1,0:T(4,128)S(1)} fusion(f32[2,512,512,4]{2,1,3,0:T(8,128)S(1)} %get-tuple-element.253, f32[2,4,512]{2,1,0:T(4,128)S(1)} %get-tuple-element.229, pred[512,512]{0,1:T(8,128)(4,1)S(1)} %get-tuple-element.244), kind=kLoop, calls=%fused_computation.16 | loop fusion | flops 10481664 | bytes 8683520 | tf_op jit(solution)/shard_map/reduce_sum | solution.py:65
  59.9 0.0 copy-done.3
  59.9 3.8 %fusion.14 = f32[2,4,512,128]{2,3,1,0:T(8,128)} fusion(bf16[512,2,128,1]{0,2,3,1:T(8,128)(2,1)S(1)} %bitcast.214, f32[2,512,512,4]{2,1,3,0:T(8,128)S(1)} %get-tuple-element.253, f32[2,4,512]{2,1,0:T(4,128)S(1)} %get-tuple-element.229, pred[512,512]{0,1:T(8,128)(4,1)S(1)} %get-tuple-element.244), kind=kOutput, calls=%fused_computation.21 | convolution fusion | flops 547356672 | bytes 11026432 | tf_op jit(solution)/shard_map/hgqk,khd->qhgd/dot_general | solution.py:66
  63.7 0.0 copy-done
  63.7 2.0 %fusion.10 = f32[2,4,512]{2,1,0:T(4,128)S(1)} fusion(f32[2,512,512,4]{2,1,3,0:T(8,128)S(1)} %get-tuple-element.251, f32[2,4,512]{2,1,0:T(4,128)S(1)} %get-tuple-element.228, pred[512,512]{0,1:T(8,128)(4,1)S(1)} %get-tuple-element.245), kind=kLoop, calls=%fused_computation.18 | loop fusion | flops 10481664 | bytes 8683520 | tf_op jit(solution)/shard_map/reduce_sum | solution.py:65
  65.8 0.0 collective-permute-done.5
  65.8 0.1 copy.33
  66.0 9.1 %fusion.25 = bf16[512,2,4,128]{0,3,2,1:T(8,128)(2,1)} fusion(f32[2,4,512,128]{2,3,1,0:T(8,128)} %fusion.14, f32[2,4,512,128]{2,3,1,0:T(8,128)} %fusion.16, f32[2,4,512,128]{2,3,1,0:T(8,128)} %fusion.18, bf16[512,2,128,1]{0,2,3,1:T(8,128)(2,1)S(1)} %bitcast.215, f32[2,512,512,4]{2,1,3,0:T(8,128)} %copy-done, f32[2,4,512]{2,1,0:T(4,128)S(1)} %get-tuple-element.228, ...), kind=kOutput, calls=%fused_computation.31 | convolution fusion | flops 552075264 | bytes 16351232 | tf_op jit(solution)/shard_map/hgqk,khd->qhgd/dot_general | solution.py:66
  75.1 0.0 all-gather.2.cloned.1.call-update
  75.1 46.6 %all-gather.2.cloned.1.call-done = bf16[512,2048]{0,1:T(8,128)(2,1)} async-done(((bf16[512,1024]{0,1:T(8,128)(2,1)}), bf16[512,2048]{0,1:T(8,128)(2,1)}) %all-gather.2.cloned.1.call-update) | async-done | bytes 2097168 | tf_op jit(solution)/shard_map/all_gather | solution.py:134
  121.7 9.9 %convolution_convert_fusion = bf16[512,2048]{1,0:T(8,128)(2,1)} fusion(bf16[512,2048]{0,1:T(8,128)(2,1)} %all-gather.2.cloned.1.call-done, bf16[2048,2048]{1,0:T(8,128)(2,1)} %param.55), kind=kOutput, calls=%fused_computation.28 | convolution fusion | flops 4296015872 | bytes 12582912 | tf_op jit(solution)/shard_map/dot_general | solution.py:133
  (6 shorter events, 0.1 us)
Async XLA Ops:
  6.5 8.5 %copy-start.1 = (bf16[512,1024]{1,0:T(8,128)(2,1)S(1)}, bf16[512,1024]{1,0:T(8,128)(2,1)}, u32[]{:S(2)}) copy-start(bf16[512,1024]{1,0:T(8,128)(2,1)} %param.51) | copy-start | bytes 3145732
  6.5 115.2 %all-gather.2.cloned.1.call-start = ((), (), s32[]{:S(2)}) async-start(), calls=%async_computation | async-start | bytes 3145728 | tf_op jit(solution)/shard_map/all_gather | solution.py:134
  11.1 15.0 %collective-permute-start = (bf16[512,256]{0,1:T(8,128)(2,1)S(1)}, bf16[512,256]{0,1:T(8,128)(2,1)}, u32[]{:S(2)}, u32[]{:S(2)}) collective-permute-start(bf16[512,256]{0,1:T(8,128)(2,1)S(1)} %bitcast.211), channel_id=1, source_target_pairs={{0,2},{2,4},{4,6},{6,8},{8,10},{10,12},{12,14},{14,16},{16,18},{18... | collective-permute-start | bytes 786440 | tf_op jit(solution)/shard_map/ppermute | solution.py:19
  13.8 9.8 %collective-permute-start.1 = (bf16[512,256]{1,0:T(8,128)(2,1)}, bf16[512,256]{1,0:T(8,128)(2,1)S(1)}, u32[]{:S(2)}, u32[]{:S(2)}) collective-permute-start(bf16[512,256]{1,0:T(8,128)(2,1)} %param.53), channel_id=1, source_target_pairs={{0,2},{2,4},{4,6},{6,8},{8,10},{10,12},{12,14},{14,16},{16,18},{18... | collective-permute-start | bytes 786440 | tf_op jit(solution)/shard_map/ppermute | solution.py:19
  24.5 7.6 %collective-permute-start.3 = (bf16[512,256]{1,0:T(8,128)(2,1)S(1)}, bf16[512,256]{1,0:T(8,128)(2,1)S(1)}, u32[]{:S(2)}, u32[]{:S(2)}) collective-permute-start(bf16[512,256]{1,0:T(8,128)(2,1)S(1)} %collective-permute-done.1), channel_id=1, source_target_pairs={{0,2},{2,4},{4,6},{6,8},{8,10},{10,12},{12,14},{14,16},{16,18},{18... | collective-permute-start | bytes 786440 | tf_op jit(solution)/shard_map/ppermute | solution.py:19
  26.1 8.1 %collective-permute-start.2 = (bf16[512,256]{0,1:T(8,128)(2,1)}, bf16[512,256]{0,1:T(8,128)(2,1)S(1)}, u32[]{:S(2)}, u32[]{:S(2)}) collective-permute-start(bf16[512,256]{0,1:T(8,128)(2,1)} %collective-permute-done), channel_id=1, source_target_pairs={{0,2},{2,4},{4,6},{6,8},{8,10},{10,12},{12,14},{14,16},{16,18},{18... | collective-permute-start | bytes 786440 | tf_op jit(solution)/shard_map/ppermute | solution.py:19
  32.9 32.9 %collective-permute-start.5 = (bf16[512,256]{1,0:T(8,128)(2,1)S(1)}, bf16[512,256]{1,0:T(8,128)(2,1)S(1)}, u32[]{:S(2)}, u32[]{:S(2)}) collective-permute-start(bf16[512,256]{1,0:T(8,128)(2,1)S(1)} %collective-permute-done.3), channel_id=1, source_target_pairs={{0,2},{2,4},{4,6},{6,8},{8,10},{10,12},{12,14},{14,16},{16,18},{18... | collective-permute-start | bytes 786440 | tf_op jit(solution)/shard_map/ppermute | solution.py:19
  34.1 8.8 %collective-permute-start.4 = (bf16[512,256]{0,1:T(8,128)(2,1)S(1)}, bf16[512,256]{0,1:T(8,128)(2,1)S(1)}, u32[]{:S(2)}, u32[]{:S(2)}) collective-permute-start(bf16[512,256]{0,1:T(8,128)(2,1)S(1)} %collective-permute-done.2), channel_id=1, source_target_pairs={{0,2},{2,4},{4,6},{6,8},{8,10},{10,12},{12,14},{14,16},{16,18},{18... | collective-permute-start | bytes 786440 | tf_op jit(solution)/shard_map/ppermute | solution.py:19
  34.7 10.3 %slice-start = ((s8[8388608]{0:T(1024)(128)(4,1)}), s8[4194304]{0:T(1024)(128)(4,1)S(1)}, s32[]{:S(2)}) async-start(s8[8388608]{0:T(1024)(128)(4,1)} %bitcast.198), calls=%async_computation.1 | async-start | bytes 8388608
  42.9 2.2 %slice-start.1 = ((s8[8388608]{0:T(1024)(128)(4,1)}), s8[4194304]{0:T(1024)(128)(4,1)S(1)}, s32[]{:S(2)}) async-start(s8[8388608]{0:T(1024)(128)(4,1)} %bitcast.198), calls=%async_computation.2 | async-start | bytes 8388608
  44.9 18.8 %copy-start = (f32[2,512,512,4]{2,1,3,0:T(8,128)}, f32[2,512,512,4]{2,1,3,0:T(8,128)S(1)}, u32[]{:S(2)}) copy-start(f32[2,512,512,4]{2,1,3,0:T(8,128)S(1)} %get-tuple-element.251) | copy-start | bytes 25165828
  47.1 3.8 %slice-start.2 = ((s8[8388608]{0:T(1024)(128)(4,1)}), s8[4194304]{0:T(1024)(128)(4,1)S(1)}, s32[]{:S(2)}) async-start(s8[8388608]{0:T(1024)(128)(4,1)} %bitcast.200), calls=%async_computation.3 | async-start | bytes 8388608
  47.1 4.9 %slice-start.3 = ((s8[8388608]{0:T(1024)(128)(4,1)}), s8[4194304]{0:T(1024)(128)(4,1)S(1)}, s32[]{:S(2)}) async-start(s8[8388608]{0:T(1024)(128)(4,1)} %bitcast.200), calls=%async_computation.4 | async-start | bytes 8388608
  51.0 3.1 %copy-start.2 = (bf16[512,256]{0,1:T(8,128)(2,1)S(1)}, bf16[512,256]{0,1:T(8,128)(2,1)}, u32[]{:S(2)}) copy-start(bf16[512,256]{0,1:T(8,128)(2,1)} %copy.27) | copy-start | bytes 786436
  57.9 2.0 %copy-start.3 = (bf16[512,256]{0,1:T(8,128)(2,1)S(1)}, bf16[512,256]{0,1:T(8,128)(2,1)}, u32[]{:S(2)}) copy-start(bf16[512,256]{0,1:T(8,128)(2,1)} %copy.30) | copy-start | bytes 786436
Sparse Core Ops, SparseCore 0:
  75.2 46.4 all-gather.1
where the time goes:
time: 139 us; the launch traced here: 138 us
  waiting for transfers between devices  52.9 us (38%)
  matrix products  45.1 us (32%)
  between operations  13.7 us (10%)
  other arithmetic  13.5 us (10%)
  local copies, waits for them, and re-layouts  7.03 us (5%)
  starting transfers between devices  6.31 us (5%)
    all_gather x1, waiting for transfers between devices, shards(): lax.all_gather(attended, 'head', axis=1, tiled=True)  46.6 us
    dot_general x4, matrix products, attend(): jnp.einsum('hgqk,khd->qhgd', weights.astype(jnp.bfloat16), shaped_value,...  20.6 us
    dot_general x4, matrix products, attend(): jnp.einsum('qhgd,khd->hgqk', shaped_query, shaped_key, preferred_element_...  14.6 us
    dot_general x1, matrix products, shards(): jnp.dot(lax.all_gather(attended, 'head', axis=1, tiled=True), out_weight,...  9.9 us
    reduce_sum x4, other arithmetic, attend(): totals = totals * factor + jnp.sum(weights, axis=3)  8.1 us
    ppermute x6, starting transfers between devices, passed_along(): return lax.ppermute(value, axis, pairs)  6.31 us
    ppermute x6, waiting for transfers between devices, passed_along(): return lax.ppermute(value, axis, pairs)  6.22 us
    unnamed x20, local copies, waits for them, and re-layouts  3.2 us
  transfers between devices with their start and end apart: 7, of which 2 were waited for; matrix products, arithmetic and copies ran while one was open for 30% of the time, Pallas kernels for 0%

commit v1 on v0

v1 whole, which is shorter than its diff:
```python
import functools
import math

import jax
import jax.numpy as jnp
import numpy as np
from jax import lax
from jax.experimental import pallas as pl
from jax.experimental.pallas import tpu as pltpu
from jax.sharding import PartitionSpec as P

HEAD = 128
STEPS = 4
MASKED = -1e30
MESH = pl.DeviceIdType.MESH

PART_1 = 1.5703125
PART_2 = 507.0 / 2.0**20
PART_3 = math.pi / 2 - PART_1 - PART_2


def cosine_and_sine(angle, lane):
    turns = jnp.floor(angle * (2.0 / math.pi) + 0.5)
    rest = ((angle - turns * PART_1) - turns * PART_2) - turns * PART_3
    quadrant = turns.astype(jnp.int32) + jnp.where(lane < HEAD // 2, 1, 0)
    z = rest * rest
    sine = ((-1.9515295891e-4 * z + 8.3321608736e-3) * z - 1.6666654611e-1) * z * rest + rest
    cosine = ((2.443315711809948e-5 * z - 1.388731625493765e-3) * z + 4.166664568298827e-2) * z * z - 0.5 * z + 1.0
    value = jnp.where((quadrant & 1) == 1, cosine, sine)
    return jnp.where((quadrant & 2) == 2, -value, value)


def kernel(
    cycle,
    q_hbm, k_hbm, v_hbm, pos_hbm, freq_hbm, w_hbm,
    out_ref,
    q_in, k_in, v_in, pos_in, freq_in, weight,
    pos_col, cos_tab, sin_tab, q_rot, own_kv, met_kv, top, total, sums, att_own, att_met, mixed,
    load_sem, kv_send, kv_recv, x_send, x_recv,
):
    block = lax.axis_index("ctx")
    head = lax.axis_index("head")
    half = q_in.shape[1] // 2
    pairs = q_in.shape[0]
    groups = own_kv.shape[1]
    wide = 2 * HEAD
    scale = math.log2(math.e) / math.sqrt(HEAD)
    even = lax.rem(block, 2) == 0
    twin = jnp.where(even, block + 1, block - 1)

    small = [
        pltpu.make_async_copy(pos_hbm, pos_in, load_sem.at[0]),
        pltpu.make_async_copy(freq_hbm, freq_in, load_sem.at[1]),
        pltpu.make_async_copy(k_hbm, k_in, load_sem.at[2]),
        pltpu.make_async_copy(v_hbm, v_in, load_sem.at[3]),
    ]
    for copy in small:
        copy.start()
    q_loads = [
        pltpu.make_async_copy(q_hbm.at[:, pl.ds(p * wide, wide)], q_in.at[p], load_sem.at[4 + p]) for p in range(pairs)
    ]
    for copy in q_loads:
        copy.start()
    rows = weight.shape[1]
    w_loads = [
        pltpu.make_async_copy(w_hbm.at[pl.ds(pl.multiple_of(head * rows, rows), rows)], weight.at[0], load_sem.at[8]),
        pltpu.make_async_copy(
            w_hbm.at[pl.ds(pl.multiple_of((1 - head) * rows, rows), rows)], weight.at[1], load_sem.at[9]
        ),
    ]
    for copy in w_loads:
        copy.start()

    def at(step):
        return (lax.rem(block + step + cycle, cycle), head)

    barrier = pltpu.get_barrier_semaphore()
    friends = [at(1), at(-1), at(3), at(-3), (block, 1 - head), (twin, head)]
    for friend in friends:
        pl.semaphore_signal(barrier, inc=1, device_id=friend, device_id_type=MESH)

    for copy in small:
        copy.wait()
    lane = lax.broadcasted_iota(jnp.int32, (HEAD, HEAD), 1)
    frequency = freq_in[0:1, :]
    for i in range(2 * half // HEAD):
        cut = pl.ds(i * HEAD, HEAD)
        column = jnp.transpose(jnp.broadcast_to(pos_in[i : i + 1, :].astype(jnp.float32), (HEAD, HEAD)))
        pos_col[cut, :] = column.astype(jnp.int32)
        both = cosine_and_sine(column * frequency, lane)
        other = pltpu.roll(both, HEAD // 2, 1)
        cos_tab[cut, :] = jnp.where(lane < HEAD // 2, both, other)
        sin_tab[cut, :] = jnp.where(lane < HEAD // 2, -other, both)

    def rotated(block_rows, cut):
        value = block_rows.astype(jnp.float32)
        return (value * cos_tab[cut, :] + pltpu.roll(value, HEAD // 2, 1) * sin_tab[cut, :]).astype(jnp.bfloat16)

    for part in range(2):
        cut = pl.ds(part * half, half)
        for group in range(groups):
            columns = pl.ds(group * HEAD, HEAD)
            own_kv[part, group, 0] = rotated(k_in[cut, columns], cut)
            own_kv[part, group, 1] = v_in[cut, columns]

    pl.semaphore_wait(barrier, len(friends))

    def kv_copy(slot, step, group):
        part = jnp.where(block + step < cycle, 0, 1)
        return pltpu.make_async_remote_copy(
            own_kv.at[part, group], met_kv.at[step - 1, group], kv_send.at[slot, group], kv_recv.at[step - 1, group],
            device_id=at(step), device_id_type=MESH,
        )

    first_step = jnp.where(even, 1, 3)
    other_step = 4 - first_step

    def hand_copy(group):
        return pltpu.make_async_remote_copy(
            met_kv.at[first_step - 1, group], met_kv.at[1, group], kv_send.at[2, group], kv_recv.at[1, group],
            device_id=(twin, head), device_id_type=MESH,
        )

    def kv_wait(step, group):
        pltpu.make_async_remote_copy(
            met_kv.at[step - 1, group], met_kv.at[step - 1, group], kv_send.at[2, group], kv_recv.at[step - 1, group],
            device_id=(twin, head), device_id_type=MESH,
        ).wait_recv()

    for group in range(groups):
        kv_copy(0, 1, group).start()
        kv_copy(1, 3, group).start()

    def x_copy(part, order, p):
        cut = pl.ds(pl.multiple_of(part * half, half), half)
        return pltpu.make_async_remote_copy(
            att_own.at[p, cut], att_met.at[p, cut], x_send.at[order, p], x_recv.at[order, p],
            device_id=(block, 1 - head), device_id_type=MESH,
        )

    first = jnp.where(block == 0, 0, 1)
    second = 1 - first
    mixing = (block == 1) | (block == 2)

    row_at = lax.broadcasted_iota(jnp.int32, (half, wide), 0)
    key_at = lax.broadcasted_iota(jnp.int32, (half, wide), 1)

    def both_lanes(value):
        return jnp.concatenate([value, value], axis=1)

    def finish(part, p):
        cut = pl.ds(pl.multiple_of(part * half, half), half)
        for i in range(2):
            sum_all = jnp.sum(total[2 * p + i, cut, :], axis=1, keepdims=True)
            att_own[p, cut, i * HEAD : (i + 1) * HEAD] = (sums[2 * p + i, cut, :] / sum_all).astype(jnp.bfloat16)

    for copy in q_loads:
        copy.wait()

    def own_block(i, carry):
        part = jnp.where(i < pairs, first, second)
        p = lax.rem(i, pairs)
        cut = pl.ds(pl.multiple_of(part * half, half), half)
        group = p // (pairs // groups)
        keys = own_kv[part, group, 0]
        values = own_kv[part, group, 1]
        reach = both_lanes(pos_col[cut, :])
        seen = (key_at <= row_at) & (key_at >= row_at - reach)
        for n in range(2):
            query = rotated(q_in[p, cut, n * HEAD : (n + 1) * HEAD], cut)
            q_rot[p, cut, n * HEAD : (n + 1) * HEAD] = query
            scores = lax.dot_general(query, keys, (((1,), (1,)), ((), ())), preferred_element_type=jnp.float32)
            scores = jnp.where(seen, scores, MASKED)
            highest = jnp.broadcast_to(jnp.max(scores, axis=1, keepdims=True), (half, HEAD))
            weights = jnp.exp2((scores - both_lanes(highest)) * scale)
            top[2 * p + n, cut, :] = highest
            total[2 * p + n, cut, :] = weights[:, :HEAD] + weights[:, HEAD:]
            sums[2 * p + n, cut, :] = jnp.dot(
                weights.astype(jnp.bfloat16), values, preferred_element_type=jnp.float32
            )

        @pl.when((i < pairs) & jnp.logical_not(mixing))
        def _():
            finish(part, p)
            x_copy(part, 0, p).start()

        return carry

    lax.fori_loop(0, 2 * pairs, own_block, 0)

    def met_block(step, group, p):
        early = step <= block
        part = jnp.where(early, 0, 1)
        apart = jnp.where(early, step, cycle - step) * half
        cut = pl.ds(pl.multiple_of(part * half, half), half)
        keys = met_kv[step - 1, group, 0]
        values = met_kv[step - 1, group, 1]
        reach = both_lanes(pos_col[cut, :])
        seen = key_at >= row_at - reach + apart
        for n in range(2):
            query = q_rot[p, cut, n * HEAD : (n + 1) * HEAD]
            scores = lax.dot_general(query, keys, (((1,), (1,)), ((), ())), preferred_element_type=jnp.float32)
            scores = jnp.where(seen, scores, MASKED)
            before = top[2 * p + n, cut, :]
            highest = jnp.maximum(before, jnp.max(scores, axis=1, keepdims=True))
            factor = jnp.exp2((before - highest) * scale)
            weights = jnp.exp2((scores - both_lanes(highest)) * scale)
            top[2 * p + n, cut, :] = highest
            total[2 * p + n, cut, :] = total[2 * p + n, cut, :] * factor + (weights[:, :HEAD] + weights[:, HEAD:])
            sums[2 * p + n, cut, :] = sums[2 * p + n, cut, :] * factor + jnp.dot(
                weights.astype(jnp.bfloat16), values, preferred_element_type=jnp.float32
            )

    tile = 512
    tiles = out_ref.shape[1] // tile

    def project(att, which, part, begin, end, fresh, last):
        cut = pl.ds(pl.multiple_of(part * half, half), half)
        row_cut = slice(begin * wide, end * wide)

        def one(t, carry):
            columns = pl.ds(pl.multiple_of(t * tile, tile), tile)
            left = jnp.concatenate([att[p, cut, :] for p in range(begin, end)], axis=1)
            value = jnp.dot(left, weight[which, row_cut, columns], preferred_element_type=jnp.float32)
            if not fresh:
                value = mixed[cut, columns] + value
            if last:
                out_ref[cut, columns] = value.astype(jnp.bfloat16)
            else:
                mixed[cut, columns] = value
            return carry

        lax.fori_loop(0, tiles, one, 0)

    per_group = pairs // groups

    def met_group(group):
        for step, known in ((first_step, True), (other_step, False), (2, False)):
            if not known:
                kv_wait(step, group)

            def one(p, carry):
                met_block(step, group, group * per_group + p)
                return carry

            lax.fori_loop(0, per_group, one, 0)
        for p in range(group * per_group, (group + 1) * per_group):
            finish(second, p)
            x_copy(second, 1, p).start()

            @pl.when(mixing)
            def _():
                finish(first, p)
                x_copy(first, 0, p).start()

    kv_wait(first_step, 0)
    hand_copy(0).start()
    met_group(0)
    kv_wait(first_step, 1)
    hand_copy(1).start()
    met_group(1)

    for copy in w_loads:
        copy.wait()
    project(att_own, 0, first, 0, pairs, True, False)
    project(att_own, 0, second, 0, pairs, True, False)
    for p in range(pairs):
        x_copy(first, 0, p).wait_recv()
    project(att_met, 1, first, 0, pairs, False, True)
    for p in range(pairs - 1):
        x_copy(second, 1, p).wait_recv()
    project(att_met, 1, second, 0, pairs - 1, False, False)
    x_copy(second, 1, pairs - 1).wait_recv()
    project(att_met, 1, second, pairs - 1, pairs, False, True)

    for p in range(pairs):
        x_copy(first, 0, p).wait_send()
        x_copy(second, 1, p).wait_send()
    for group in range(groups):
        kv_copy(0, 1, group).wait_send()
        kv_copy(1, 3, group).wait_send()
        hand_copy(group).wait_send()


def shards(queries, keys, values, positions, out_weight):
    number, width = queries.shape
    half = number // 2
    pairs = width // (2 * HEAD)
    groups = keys.shape[1] // HEAD
    heads = width // HEAD
    columns = out_weight.shape[1]
    cycle = lax.axis_size("ctx")
    table = np.power(500000.0, -2.0 * np.arange(HEAD // 2) / HEAD).astype(np.float32)
    frequency = jnp.asarray(np.tile(np.concatenate([table, table])[None, :], (8, 1)))
    f32, bf16, i32 = jnp.float32, jnp.bfloat16, jnp.int32
    hbm = pl.BlockSpec(memory_space=pltpu.MemorySpace.HBM)
    return pl.pallas_call(
        functools.partial(kernel, cycle),
        name="attend_and_project",
        out_shape=jax.ShapeDtypeStruct((number, columns), bf16),
        in_specs=[hbm] * 6,
        out_specs=pl.BlockSpec(memory_space=pltpu.MemorySpace.VMEM),
        scratch_shapes=[
            pltpu.VMEM((pairs, number, 2 * HEAD), bf16),
            pltpu.VMEM((number, groups * HEAD), bf16),
            pltpu.VMEM((number, groups * HEAD), bf16),
            pltpu.VMEM((number // HEAD, HEAD), i32),
            pltpu.VMEM((8, HEAD), f32),
            pltpu.VMEM((2, width, columns), bf16),
            pltpu.VMEM((number, HEAD), i32),
            pltpu.VMEM((number, HEAD), f32),
            pltpu.VMEM((number, HEAD), f32),
            pltpu.VMEM((pairs, number, 2 * HEAD), bf16),
            pltpu.VMEM((2, groups, 2, half, HEAD), bf16),
            pltpu.VMEM((STEPS - 1, groups, 2, half, HEAD), bf16),
            pltpu.VMEM((heads, number, HEAD), f32),
            pltpu.VMEM((heads, number, HEAD), f32),
            pltpu.VMEM((heads, number, HEAD), f32),
            pltpu.VMEM((pairs, number, 2 * HEAD), bf16),
            pltpu.VMEM((pairs, number, 2 * HEAD), bf16),
            pltpu.VMEM((number, columns), f32),
            pltpu.SemaphoreType.DMA((10,)),
            pltpu.SemaphoreType.DMA((STEPS - 1, groups)),
            pltpu.SemaphoreType.DMA((STEPS - 1, groups)),
            pltpu.SemaphoreType.DMA((2, pairs)),
            pltpu.SemaphoreType.DMA((2, pairs)),
        ],
        compiler_params=pltpu.CompilerParams(collective_id=0, has_side_effects=True, vmem_limit_bytes=61 << 20),
    )(queries, keys, values, positions.reshape(number // HEAD, HEAD), frequency, out_weight)


def solution(mesh):
    in_specs = (P("ctx", "head"), P("ctx", "head"), P("ctx", "head"), P("ctx"), P(None, "head"))
    out_specs = P("ctx", "head")
    return jax.shard_map(shards, mesh=mesh, in_specs=in_specs, out_specs=out_specs, check_vma=False)
```

time: 139 us -> 51 us (0.37)
  waiting for transfers between devices: 52.9 us -> 0 us
  Pallas kernels: 0 us -> 47.7 us
  matrix products: 45.1 us -> 0 us
  between operations: 13.7 us -> 0.01 us
  other arithmetic: 13.5 us -> 0 us
  starting transfers between devices: 6.31 us -> 0 us
  local copies, waits for them, and re-layouts: 7.03 us -> 3.16 us
    pallas_call x0 -> x1, Pallas kernels: none -> 47.7 us  [shards(): pl.pallas_call(functools.partial(kernel, cycle), name='attend_and_project...]
    all_gather x1 -> x0, waiting for transfers between devices: 46.6 us -> none  [shards(): lax.all_gather(attended, 'head', axis=1, tiled=True)]
    dot_general x9 -> x0, matrix products: 45.1 us -> none  [the longest x4 20.6 us: attend(): jnp.einsum('hgqk,khd->qhgd', weights.astype(jnp.bfloat16), shaped_value,...]
    reduce_sum x4 -> x0, other arithmetic: 8.1 us -> none  [attend(): totals = totals * factor + jnp.sum(weights, axis=3)]
    ppermute x6 -> x0, starting transfers between devices: 6.31 us -> none  [passed_along(): return lax.ppermute(value, axis, pairs)]
    ppermute x6 -> x0, waiting for transfers between devices: 6.22 us -> none  [passed_along(): return lax.ppermute(value, axis, pairs)]
    ppermute x3 -> x0, local copies, waits for them, and re-layouts: 1.85 us -> none  [passed_along(): return lax.ppermute(value, axis, pairs)]
    cos x1 -> x0, other arithmetic: 1.63 us -> none  [rotate(): cosine = jnp.cos(angle)[:, None, :]]
  transfers between devices with their start and end apart: 7 -> 0, of which waited for: 2 -> 0; matrix products, arithmetic and copies ran while one was open for 30% -> 0% of each run, Pallas kernels for 0% -> 0%
where the time goes in v1:
time: 51 us; the launch traced here: 50.9 us
  Pallas kernels  47.7 us (94%)
  local copies, waits for them, and re-layouts  3.16 us (6%)
    pallas_call x1, Pallas kernels, shards(): pl.pallas_call(functools.partial(kernel, cycle), name='attend_and_project...  47.7 us
    unnamed x1, local copies, waits for them, and re-layouts  3.16 us

profile of v1, /device:TPU:1, one launch (start us, length us, event | category | flops | bytes accessed | tf_op | source)
XLA Modules:
  0.0 50.9 jit_solution(1048526194614545595)
XLA Ops:
  0.0 47.7 %attend_and_project.1 = bf16[512,2048]{1,0:T(8,128)(2,1)} custom-call(bf16[512,1024]{1,0:T(8,128)(2,1)} %q_hbm.1, bf16[512,256]{1,0:T(8,128)(2,1)} %k_hbm.1, bf16[512,256]{1,0:T(8,128)(2,1)} %v_hbm.1, s32[4,128]{1,0:T(4,128)} %bitcast.1, f32[8,128]{1,0:T(8,128)} %constant.2.clone.freq_hbm, bf16[2048,2048]{1,0:T(8,128)(2,1)} %w_hbm.1), custom_call_target="tpu_custom_call" | custom-call | tf_op jit(solution)/shard_map/attend_and_project/pallas_call | solution.py:297
  47.7 3.2 %copy.8 = bf16[512,2048]{1,0:T(8,128)(2,1)} copy(bf16[512,2048]{1,0:T(8,128)(2,1)} %attend_and_project.1) | data formatting | bytes 4194304

commit v2 on v1

v2 whole, which is shorter than its diff:
```python
import functools
import math

import jax
import jax.numpy as jnp
import numpy as np
from jax import lax
from jax.experimental import pallas as pl
from jax.experimental.pallas import tpu as pltpu
from jax.sharding import PartitionSpec as P

HEAD = 128
STEPS = 4
MASKED = -1e30
MESH = pl.DeviceIdType.MESH

PART_1 = 1.5703125
PART_2 = 507.0 / 2.0**20
PART_3 = math.pi / 2 - PART_1 - PART_2


def cosine_and_sine(angle, lane):
    turns = jnp.floor(angle * (2.0 / math.pi) + 0.5)
    rest = ((angle - turns * PART_1) - turns * PART_2) - turns * PART_3
    quadrant = turns.astype(jnp.int32) + jnp.where(lane < HEAD // 2, 1, 0)
    z = rest * rest
    sine = ((-1.9515295891e-4 * z + 8.3321608736e-3) * z - 1.6666654611e-1) * z * rest + rest
    cosine = ((2.443315711809948e-5 * z - 1.388731625493765e-3) * z + 4.166664568298827e-2) * z * z - 0.5 * z + 1.0
    value = jnp.where((quadrant & 1) == 1, cosine, sine)
    return jnp.where((quadrant & 2) == 2, -value, value)


def kernel(
    cycle,
    q_hbm, k_hbm, v_hbm, pos_hbm, freq_hbm, w_hbm,
    out_ref,
    q_in, k_in, v_in, pos_in, freq_in, weight,
    pos_col, cos_tab, sin_tab, q_rot, own_k, own_v, met_k, met_v, top, total, sums, att_own, att_met, mixed,
    load_sem, kv_send, kv_recv, x_send, x_recv,
):
    block = lax.axis_index("ctx")
    head = lax.axis_index("head")
    half = q_in.shape[1] // 2
    pairs = q_in.shape[0]
    groups = own_k.shape[1]
    wide = 2 * HEAD
    scale = math.log2(math.e) / math.sqrt(HEAD)
    even = lax.rem(block, 2) == 0
    twin = jnp.where(even, block + 1, block - 1)

    small = [
        pltpu.make_async_copy(pos_hbm, pos_in, load_sem.at[0]),
        pltpu.make_async_copy(freq_hbm, freq_in, load_sem.at[1]),
        pltpu.make_async_copy(k_hbm, k_in, load_sem.at[2]),
        pltpu.make_async_copy(v_hbm, v_in, load_sem.at[3]),
    ]
    for copy in small:
        copy.start()
    q_loads = [
        pltpu.make_async_copy(q_hbm.at[:, pl.ds(p * wide, wide)], q_in.at[p], load_sem.at[4 + p]) for p in range(pairs)
    ]
    for copy in q_loads:
        copy.start()
    rows = weight.shape[1]
    w_loads = [
        pltpu.make_async_copy(w_hbm.at[pl.ds(pl.multiple_of(head * rows, rows), rows)], weight.at[0], load_sem.at[8]),
        pltpu.make_async_copy(
            w_hbm.at[pl.ds(pl.multiple_of((1 - head) * rows, rows), rows)], weight.at[1], load_sem.at[9]
        ),
    ]

    def at(step):
        return (lax.rem(block + step + cycle, cycle), head)

    place = lax.rem(block, 8)
    last = {1: (place == 7) & (block < cycle - 1), 3: place == 7}
    relay = ((place == 1) & (block + 7 < cycle)) | (place == 3)
    origin = at(jnp.where(place == 1, 6, 4))

    def goal(step):
        return at(jnp.where(last[step], step - 7, step))

    barrier = pltpu.get_barrier_semaphore()
    senders = [
        at(jnp.where((place == 0) & (block > 0), -7, -1)), at(jnp.where(place == 2, -7, -3)), (block, 1 - head), (twin, head),
    ]
    for friend in senders:
        pl.semaphore_signal(barrier, inc=1, device_id=friend, device_id_type=MESH)

    @pl.when(relay)
    def _():
        pl.semaphore_signal(barrier, inc=1, device_id=origin, device_id_type=MESH)

    VALUES = groups

    def own_piece(part, piece):
        return own_k.at[part, piece] if piece < VALUES else own_v.at[part]

    def met_piece(slot, piece):
        return met_k.at[slot, piece] if piece < VALUES else met_v.at[slot]

    def kv_copy(slot, step, piece):
        part = jnp.where(block + step < cycle, 0, 1)
        there = jnp.where(last[step], STEPS - 1, step - 1)
        return pltpu.make_async_remote_copy(
            own_piece(part, piece), met_piece(there, piece), kv_send.at[slot, piece], kv_recv.at[there, piece],
            device_id=goal(step), device_id_type=MESH,
        )

    def kv_start(piece):
        kv_copy(0, 1, piece).start()
        kv_copy(1, 3, piece).start()

    first_step = jnp.where(even, 1, 3)
    other_step = 4 - first_step

    def hand_copy(piece):
        return pltpu.make_async_remote_copy(
            met_piece(first_step - 1, piece), met_piece(1, piece), kv_send.at[2, piece], kv_recv.at[1, piece],
            device_id=(twin, head), device_id_type=MESH,
        )

    def relay_copy(piece):
        there = jnp.where(place == 1, 0, 2)
        return pltpu.make_async_remote_copy(
            met_piece(STEPS - 1, piece), met_piece(there, piece), kv_send.at[3, piece], kv_recv.at[there, piece],
            device_id=at(7), device_id_type=MESH,
        )

    def kv_wait(slot, piece):
        pltpu.make_async_remote_copy(
            met_piece(slot, piece), met_piece(slot, piece), kv_send.at[2, piece], kv_recv.at[slot, piece],
            device_id=(twin, head), device_id_type=MESH,
        ).wait_recv()

    for copy in small[3:]:
        copy.wait()
    for part in range(2):
        for group in range(groups):
            own_v[part, group] = v_in[pl.ds(part * half, half), pl.ds(group * HEAD, HEAD)]
    pl.semaphore_wait(barrier, jnp.where(relay, 5, 4))
    kv_start(VALUES)

    for copy in small[:3]:
        copy.wait()
    lane = lax.broadcasted_iota(jnp.int32, (HEAD, HEAD), 1)
    frequency = freq_in[0:1, :]

    def rotated(block_rows, cut):
        value = block_rows.astype(jnp.float32)
        return (value * cos_tab[cut, :] + pltpu.roll(value, HEAD // 2, 1) * sin_tab[cut, :]).astype(jnp.bfloat16)

    def prepare(part):
        for i in range(half // HEAD):
            cut = pl.ds(pl.multiple_of(part * half + i * HEAD, HEAD), HEAD)
            line = pos_in[pl.ds(part * (half // HEAD) + i, 1), :].astype(jnp.float32)
            column = jnp.transpose(jnp.broadcast_to(line, (HEAD, HEAD)))
            pos_col[cut, :] = column.astype(jnp.int32)
            both = cosine_and_sine(column * frequency, lane)
            other = pltpu.roll(both, HEAD // 2, 1)
            cos_tab[cut, :] = jnp.where(lane < HEAD // 2, both, other)
            sin_tab[cut, :] = jnp.where(lane < HEAD // 2, -other, both)
        cut = pl.ds(pl.multiple_of(part * half, half), half)
        for group in range(groups):
            own_k[part, group] = rotated(k_in[cut, pl.ds(group * HEAD, HEAD)], cut)

    def x_copy(part, order, p):
        cut = pl.ds(pl.multiple_of(part * half, half), half)
        return pltpu.make_async_remote_copy(
            att_own.at[p, cut], att_met.at[p, cut], x_send.at[order, p], x_recv.at[order, p],
            device_id=(block, 1 - head), device_id_type=MESH,
        )

    far = block < STEPS - 1

    first = jnp.where(far, 0, 1)
    second = 1 - first
    alone = jnp.logical_not(far) | (block == 0)

    row_at = lax.broadcasted_iota(jnp.int32, (half, wide), 0)
    key_at = lax.broadcasted_iota(jnp.int32, (half, wide), 1)
    per_group = pairs // groups

    def both_lanes(value):
        return jnp.concatenate([value, value], axis=1)

    def finish(part, p):
        cut = pl.ds(pl.multiple_of(part * half, half), half)
        for n in range(2):
            share = 1.0 / jnp.sum(total[2 * p + n, cut, :], axis=1, keepdims=True)
            att_own[p, cut, n * HEAD : (n + 1) * HEAD] = (sums[2 * p + n, cut, :] * share).astype(jnp.bfloat16)

    def own_block(part, p):
        cut = pl.ds(pl.multiple_of(part * half, half), half)
        group = p // per_group
        keys = own_k[part, group]
        values = own_v[part, group]
        reach = both_lanes(pos_col[cut, :])
        seen = (key_at <= row_at) & (key_at >= row_at - reach)
        for m in range(2):
            lanes = slice(m * HEAD, (m + 1) * HEAD)
            h = 2 * p + m
            query = rotated(q_in[p, cut, lanes], cut)
            q_rot[p, cut, lanes] = query
            scores = lax.dot_general(query, keys, (((1,), (1,)), ((), ())), preferred_element_type=jnp.float32)
            scores = jnp.where(seen, scores, MASKED)
            highest = jnp.broadcast_to(jnp.max(scores, axis=1, keepdims=True), (half, HEAD))
            weights = jnp.exp2((scores - both_lanes(highest)) * scale)
            top[h, cut, :] = highest
            total[h, cut, :] = weights[:, :HEAD] + weights[:, HEAD:]
            sums[h, cut, :] = jnp.dot(weights.astype(jnp.bfloat16), values, preferred_element_type=jnp.float32)

    def first_own(p, carry):
        own_block(first, p)

        @pl.when(alone)
        def _():
            finish(first, p)
            x_copy(first, 0, p).start()

        @pl.when(p == 0)
        def _():
            prepare(second)
            for piece in range(groups):
                kv_start(piece)

        @pl.when(relay & (p == 1))
        def _():
            for piece in (VALUES, *range(groups)):
                kv_wait(STEPS - 1, piece)
                relay_copy(piece).start()

        return carry

    def second_own(group, carry):
        for m in range(per_group):
            own_block(second, group * per_group + m)
        return carry

    prepare(first)
    for copy in q_loads:
        copy.wait()
    for copy in w_loads:
        copy.start()
    lax.fori_loop(0, pairs, first_own, 0)
    lax.fori_loop(0, groups, second_own, 0)

    def met_block(step, group):
        early = step <= block
        part = jnp.where(early, 0, 1)
        apart = jnp.where(early, step, cycle - step) * half
        cut = pl.ds(pl.multiple_of(part * half, half), half)
        keys = met_k[step - 1, group]
        values = met_v[step - 1, group]
        reach = both_lanes(pos_col[cut, :])
        seen = key_at >= row_at - reach + apart
        for m in range(2 * per_group):
            p = group * per_group + m // 2
            lanes = slice((m % 2) * HEAD, (m % 2 + 1) * HEAD)
            h = 2 * group * per_group + m
            query = q_rot[p, cut, lanes]
            scores = lax.dot_general(query, keys, (((1,), (1,)), ((), ())), preferred_element_type=jnp.float32)
            scores = jnp.where(seen, scores, MASKED)
            before = top[h, cut, :]
            highest = jnp.maximum(before, jnp.max(scores, axis=1, keepdims=True))
            factor = jnp.exp2((before - highest) * scale)
            weights = jnp.exp2((scores - both_lanes(highest)) * scale)
            top[h, cut, :] = highest
            total[h, cut, :] = total[h, cut, :] * factor + (weights[:, :HEAD] + weights[:, HEAD:])
            sums[h, cut, :] = sums[h, cut, :] * factor + jnp.dot(
                weights.astype(jnp.bfloat16), values, preferred_element_type=jnp.float32
            )
        return part

    def pick(i, usual, one, two):
        def listed(values):
            value = jnp.int32(values[-1])
            for n in range(len(values) - 1):
                value = jnp.where(i == n, values[n], value)
            return value

        return jnp.where(block == 1, listed(one), jnp.where(block == 2, listed(two), listed(usual)))

    usual_steps = (
        jnp.where(place == 0, other_step, first_step),
        jnp.where(place == 0, first_step, jnp.where(place == 2, 2, other_step)),
        jnp.where(place == 2, other_step, 2),
    )

    def meeting(i, carry):
        group = pick(i, (0, 0, 0, 1, 1, 1), (0, 1, 0, 0, 1, 1), (0, 0, 1, 1, 0, 1))
        turn = pick(i, (-1, -2, -3, -1, -2, -3), (1, 1, 3, 2, 3, 2), (1, 2, 1, 2, 3, 3))
        step = turn
        for n in range(STEPS - 1):
            step = jnp.where(turn == -1 - n, usual_steps[n], step)
        done = pick(i, (0, 0, 1, 0, 0, 1), (1, 1, 0, 1, 0, 1), (0, 1, 0, 1, 1, 1))
        handing = step == first_step

        def arrive(piece):
            kv_wait(step - 1, piece)
            pl.when(handing)(lambda: hand_copy(piece).start())

        for known in range(groups):
            pl.when(group == known)(lambda: arrive(known))
        pl.when(group == 0)(lambda: arrive(VALUES))
        part = met_block(step, group)

        @pl.when(done == 1)
        def _():
            for m in range(per_group):
                p = group * per_group + m
                finish(part, p)
                x_copy(part, jnp.where(part == first, 0, 1), p).start()

        return carry

    lax.fori_loop(0, 2 * (STEPS - 1), meeting, 0)

    tile = 256
    tiles = out_ref.shape[1] // tile

    def project(part, own, met, fresh, last):
        cut = pl.ds(pl.multiple_of(part * half, half), half)

        for t in range(tiles):
            columns = slice(t * tile, (t + 1) * tile)
            value = None if fresh else mixed[cut, columns]
            for which, att, (begin, end) in ((0, att_own, own), (1, att_met, met)):
                if begin < end:
                    left = jnp.concatenate([att[p, cut, :] for p in range(begin, end)], axis=1)
                    right = weight[which, begin * wide : end * wide, columns]
                    more = jnp.dot(left, right, preferred_element_type=jnp.float32)
                    value = more if value is None else value + more
            if last:
                out_ref[cut, columns] = value.astype(jnp.bfloat16)
            else:
                mixed[cut, columns] = value

    for copy in w_loads:
        copy.wait()
    for p in range(pairs):
        x_copy(first, 0, p).wait_recv()
    project(first, (0, pairs), (0, pairs), True, True)
    for p in range(per_group):
        x_copy(second, 1, p).wait_recv()
    project(second, (0, pairs), (0, per_group), True, False)
    for p in range(per_group, pairs):
        x_copy(second, 1, p).wait_recv()
        project(second, (0, 0), (p, p + 1), False, p == pairs - 1)

    for p in range(pairs):
        x_copy(first, 0, p).wait_send()
        x_copy(second, 1, p).wait_send()
    for piece in range(groups + 1):
        kv_copy(0, 1, piece).wait_send()
        kv_copy(1, 3, piece).wait_send()
        hand_copy(piece).wait_send()

    @pl.when(relay)
    def _():
        for piece in range(groups + 1):
            relay_copy(piece).wait_send()


def store(value_ref, out_hbm, sem):
    rows = value_ref.shape[0] // sem.shape[0]
    copies = [
        pltpu.make_async_copy(value_ref.at[pl.ds(i * rows, rows)], out_hbm.at[pl.ds(i * rows, rows)], sem.at[i])
        for i in range(sem.shape[0])
    ]
    for copy in copies:
        copy.start()
    for copy in copies:
        copy.wait()


def shards(queries, keys, values, positions, out_weight):
    number, width = queries.shape
    half = number // 2
    pairs = width // (2 * HEAD)
    groups = keys.shape[1] // HEAD
    heads = width // HEAD
    columns = out_weight.shape[1]
    cycle = lax.axis_size("ctx")
    table = np.power(500000.0, -2.0 * np.arange(HEAD // 2) / HEAD).astype(np.float32)
    frequency = jnp.asarray(np.tile(np.concatenate([table, table])[None, :], (8, 1)))
    f32, bf16, i32 = jnp.float32, jnp.bfloat16, jnp.int32
    hbm = pl.BlockSpec(memory_space=pltpu.MemorySpace.HBM)
    projected = pl.pallas_call(
        functools.partial(kernel, cycle),
        name="attend_and_project",
        out_shape=pltpu.VMEM((number, columns), bf16),
        in_specs=[hbm] * 6,
        out_specs=pl.BlockSpec(memory_space=pltpu.MemorySpace.VMEM),
        scratch_shapes=[
            pltpu.VMEM((pairs, number, 2 * HEAD), bf16),
            pltpu.VMEM((number, groups * HEAD), bf16),
            pltpu.VMEM((number, groups * HEAD), bf16),
            pltpu.VMEM((number // HEAD, HEAD), i32),
            pltpu.VMEM((8, HEAD), f32),
            pltpu.VMEM((2, width, columns), bf16),
            pltpu.VMEM((number, HEAD), i32),
            pltpu.VMEM((number, HEAD), f32),
            pltpu.VMEM((number, HEAD), f32),
            pltpu.VMEM((pairs, number, 2 * HEAD), bf16),
            pltpu.VMEM((2, groups, half, HEAD), bf16),
            pltpu.VMEM((2, groups, half, HEAD), bf16),
            pltpu.VMEM((STEPS, groups, half, HEAD), bf16),
            pltpu.VMEM((STEPS, groups, half, HEAD), bf16),
            pltpu.VMEM((heads, number, HEAD), f32),
            pltpu.VMEM((heads, number, HEAD), f32),
            pltpu.VMEM((heads, number, HEAD), f32),
            pltpu.VMEM((pairs, number, 2 * HEAD), bf16),
            pltpu.VMEM((pairs, number, 2 * HEAD), bf16),
            pltpu.VMEM((number, columns), f32),
            pltpu.SemaphoreType.DMA((10,)),
            pltpu.SemaphoreType.DMA((STEPS, groups + 1)),
            pltpu.SemaphoreType.DMA((STEPS, groups + 1)),
            pltpu.SemaphoreType.DMA((2, pairs)),
            pltpu.SemaphoreType.DMA((2, pairs)),
        ],
        compiler_params=pltpu.CompilerParams(collective_id=0, has_side_effects=True, vmem_limit_bytes=60 << 20),
    )(queries, keys, values, positions.reshape(number // HEAD, HEAD), frequency, out_weight)
    return pl.pallas_call(
        store,
        name="store",
        out_shape=jax.ShapeDtypeStruct((number, columns), bf16),
        in_specs=[pl.BlockSpec(memory_space=pltpu.MemorySpace.VMEM)],
        out_specs=pl.BlockSpec(memory_space=pltpu.MemorySpace.HBM),
        scratch_shapes=[pltpu.SemaphoreType.DMA((8,))],
    )(pltpu.with_memory_space_constraint(projected, pltpu.MemorySpace.VMEM))


def solution(mesh):
    in_specs = (P("ctx", "head"), P("ctx", "head"), P("ctx", "head"), P("ctx"), P(None, "head"))
    out_specs = P("ctx", "head")
    return jax.shard_map(shards, mesh=mesh, in_specs=in_specs, out_specs=out_specs, check_vma=False)
```

time: 51 us -> 38.3 us (0.75)
  Pallas kernels: 47.7 us -> 38.2 us
  local copies, waits for them, and re-layouts: 3.16 us -> 0 us
    pallas_call x1, Pallas kernels: 47.7 us -> 36.8 us  [shards(): pl.pallas_call(functools.partial(kernel, cycle), name='attend_and_project...]
    unnamed x1 -> x0, local copies, waits for them, and re-layouts: 3.16 us -> none
    pallas_call x0 -> x1, Pallas kernels: none -> 1.38 us  [shards(): pl.pallas_call(store, name='store', out_shape=jax.ShapeDtypeStruct((numbe...]
where the time goes in v2:
time: 38.3 us; the launch traced here: 38.2 us
  Pallas kernels  38.2 us (100%)
    pallas_call x1, Pallas kernels, shards(): pl.pallas_call(functools.partial(kernel, cycle), name='attend_and_project...  36.8 us
    pallas_call x1, Pallas kernels, shards(): pl.pallas_call(store, name='store', out_shape=jax.ShapeDtypeStruct((numbe...  1.38 us

profile of v2, /device:TPU:1, one launch (start us, length us, event | category | flops | bytes accessed | tf_op | source)
XLA Modules:
  0.0 38.2 jit_solution(11736094110731164788)
XLA Ops:
  0.0 36.8 %attend_and_project.1.value_ref = bf16[512,2048]{1,0:T(8,128)(2,1)S(1)} custom-call(bf16[512,1024]{1,0:T(8,128)(2,1)} %q_hbm.1, bf16[512,256]{1,0:T(8,128)(2,1)} %k_hbm.1, bf16[512,256]{1,0:T(8,128)(2,1)} %v_hbm.1, s32[4,128]{1,0:T(4,128)} %bitcast.1, f32[8,128]{1,0:T(8,128)} %constant.2.clone.freq_hbm, bf16[2048,2048]{1,0:T(8,128)(2,1)} %w_hbm.1), custom_call_target="tpu_custom_call" | custom-call | tf_op jit(solution)/shard_map/attend_and_project/pallas_call | solution.py:389
  36.8 1.4 %store.1 = bf16[512,2048]{1,0:T(8,128)(2,1)} custom-call(bf16[512,2048]{1,0:T(8,128)(2,1)S(1)} %attend_and_project.1.value_ref), custom_call_target="tpu_custom_call" | custom-call | tf_op jit(solution)/shard_map/store/pallas_call | solution.py:424

commit v3 on v2

--- a/solution.py
+++ b/solution.py
@@ -36,7 +36,7 @@
     out_ref,
     q_in, k_in, v_in, pos_in, freq_in, weight,
     pos_col, cos_tab, sin_tab, q_rot, own_k, own_v, met_k, met_v, top, total, sums, att_own, att_met, mixed,
-    load_sem, kv_send, kv_recv, x_send, x_recv,
+    load_sem, kv_send, kv_recv, x_send, x_recv, ready,
 ):
     block = lax.axis_index("ctx")
     head = lax.axis_index("head")
@@ -73,43 +73,75 @@
         return (lax.rem(block + step + cycle, cycle), head)
 
     place = lax.rem(block, 8)
-    last = {1: (place == 7) & (block < cycle - 1), 3: place == 7}
-    relay = ((place == 1) & (block + 7 < cycle)) | (place == 3)
-    origin = at(jnp.where(place == 1, 6, 4))
-
-    def goal(step):
-        return at(jnp.where(last[step], step - 7, step))
+    relay_one = place < 2
+    relay_all = place == 3
+    relay = relay_one | relay_all
+    forth = jnp.where(relay_one, 8, 7)
+    origin = jnp.where(place == 0, 7, jnp.where(place == 1, 5, 4))
+    wrapped = relay & (block + forth >= cycle)
+    fed_from = jnp.where(place == 2, -7, -8)
+    fed = (place <= 2) & (block >= 8)
+
+    def passes(step, piece):
+        by_relay = (place == 7) if step == 3 else jnp.bool_(False)
+        return by_relay | (place == 7) | ((place == 6) & (step == 3)) if piece >= 2 else by_relay
+
+    def goal(step, piece):
+        back = jnp.where((place == 7) & (step == 3), 7, 8)
+        return at(jnp.where(passes(step, piece), step - back, step))
 
     barrier = pltpu.get_barrier_semaphore()
-    senders = [
-        at(jnp.where((place == 0) & (block > 0), -7, -1)), at(jnp.where(place == 2, -7, -3)), (block, 1 - head), (twin, head),
-    ]
-    for friend in senders:
-        pl.semaphore_signal(barrier, inc=1, device_id=friend, device_id_type=MESH)
+
+    def signal(semaphore, device):
+        pl.semaphore_signal(semaphore, inc=1, device_id=device, device_id_type=MESH)
+
+    for friend in (at(-1), (block, 1 - head), (twin, head)):
+        signal(barrier, friend)
+    pl.when(place != 2)(lambda: signal(barrier, at(-3)))
+    pl.when((place <= 2) & (block < 8))(lambda: signal(barrier, at(fed_from)))
 
     @pl.when(relay)
     def _():
-        pl.semaphore_signal(barrier, inc=1, device_id=origin, device_id_type=MESH)
-
-    VALUES = groups
+        signal(barrier, at(origin))
+        pl.when(jnp.logical_not(wrapped))(lambda: signal(barrier, at(forth)))
+
+    def enter():
+        count = jnp.where(place >= 6, 5, 4) + jnp.where(fed, 1, 0) + jnp.where(wrapped, 1, 0)
+        pl.semaphore_wait(barrier, count)
+        pl.when(fed)(lambda: signal(ready, at(fed_from)))
 
     def own_piece(part, piece):
-        return own_k.at[part, piece] if piece < VALUES else own_v.at[part]
+        return own_k.at[part, piece // 2] if piece % 2 else own_v.at[part, piece // 2]
 
     def met_piece(slot, piece):
-        return met_k.at[slot, piece] if piece < VALUES else met_v.at[slot]
+        return met_k.at[slot, piece // 2] if piece % 2 else met_v.at[slot, piece // 2]
 
     def kv_copy(slot, step, piece):
-        part = jnp.where(block + step < cycle, 0, 1)
-        there = jnp.where(last[step], STEPS - 1, step - 1)
+        part = sent_part(step)
+        there = jnp.where(passes(step, piece), STEPS - 1, step - 1)
         return pltpu.make_async_remote_copy(
             own_piece(part, piece), met_piece(there, piece), kv_send.at[slot, piece], kv_recv.at[there, piece],
-            device_id=goal(step), device_id_type=MESH,
+            device_id=goal(step, piece), device_id_type=MESH,
         )
 
-    def kv_start(piece):
-        kv_copy(0, 1, piece).start()
-        kv_copy(1, 3, piece).start()
+    def sent_part(step):
+        return jnp.where(block + step < cycle, 0, 1)
+
+    def keys_start(part):
+        both = (sent_part(1) == part) & (sent_part(3) == part)
+
+        @pl.when(both)
+        def _():
+            for piece in range(1, 2 * groups):
+                kv_copy(0, 1, piece).start()
+                kv_copy(1, 3, piece).start()
+
+        for step in (1, 3):
+
+            @pl.when((sent_part(step) == part) & jnp.logical_not(both))
+            def _():
+                for piece in range(1, 2 * groups):
+                    kv_copy(step // 2, step, piece).start()
 
     first_step = jnp.where(even, 1, 3)
     other_step = 4 - first_step
@@ -121,10 +153,10 @@
         )
 
     def relay_copy(piece):
-        there = jnp.where(place == 1, 0, 2)
+        there = jnp.where(place == 0, 0, 2)
         return pltpu.make_async_remote_copy(
             met_piece(STEPS - 1, piece), met_piece(there, piece), kv_send.at[3, piece], kv_recv.at[there, piece],
-            device_id=at(7), device_id_type=MESH,
+            device_id=at(forth), device_id_type=MESH,
         )
 
     def kv_wait(slot, piece):
@@ -138,9 +170,6 @@
     for part in range(2):
         for group in range(groups):
             own_v[part, group] = v_in[pl.ds(part * half, half), pl.ds(group * HEAD, HEAD)]
-    pl.semaphore_wait(barrier, jnp.where(relay, 5, 4))
-    kv_start(VALUES)
-
     for copy in small[:3]:
         copy.wait()
     lane = lax.broadcasted_iota(jnp.int32, (HEAD, HEAD), 1)
@@ -210,6 +239,10 @@
             total[h, cut, :] = weights[:, :HEAD] + weights[:, HEAD:]
             sums[h, cut, :] = jnp.dot(weights.astype(jnp.bfloat16), values, preferred_element_type=jnp.float32)
 
+    def pass_on(piece):
+        kv_wait(STEPS - 1, piece)
+        relay_copy(piece).start()
+
     def first_own(p, carry):
         own_block(first, p)
 
@@ -221,23 +254,33 @@
         @pl.when(p == 0)
         def _():
             prepare(second)
-            for piece in range(groups):
-                kv_start(piece)
-
-        @pl.when(relay & (p == 1))
-        def _():
-            for piece in (VALUES, *range(groups)):
-                kv_wait(STEPS - 1, piece)
-                relay_copy(piece).start()
+            keys_start(second)
+
+        @pl.when(relay_all & (p == pairs - 2))
+        def _():
+            pl.when(jnp.logical_not(wrapped))(lambda: pl.semaphore_wait(ready, 1))
+            pass_on(0)
 
         return carry
 
     def second_own(group, carry):
         for m in range(per_group):
             own_block(second, group * per_group + m)
+
+        @pl.when(relay & (group == 0))
+        def _():
+            pl.when(relay_all)(lambda: pass_on(1))
+            pl.when(relay_one & jnp.logical_not(wrapped))(lambda: pl.semaphore_wait(ready, 1))
+            for piece in range(2, 2 * groups):
+                pass_on(piece)
+
         return carry
 
     prepare(first)
+    enter()
+    kv_copy(0, 1, 0).start()
+    kv_copy(1, 3, 0).start()
+    keys_start(first)
     for copy in q_loads:
         copy.wait()
     for copy in w_loads:
@@ -281,28 +324,30 @@
 
         return jnp.where(block == 1, listed(one), jnp.where(block == 2, listed(two), listed(usual)))
 
-    usual_steps = (
-        jnp.where(place == 0, other_step, first_step),
-        jnp.where(place == 0, first_step, jnp.where(place == 2, 2, other_step)),
-        jnp.where(place == 2, other_step, 2),
-    )
+    def usual_steps(group):
+        late = (place < 2) & (group == 1)
+        return (
+            jnp.where(late, other_step, first_step),
+            jnp.where(late, first_step, jnp.where(place == 2, 2, other_step)),
+            jnp.where(place == 2, other_step, 2),
+        )
 
     def meeting(i, carry):
         group = pick(i, (0, 0, 0, 1, 1, 1), (0, 1, 0, 0, 1, 1), (0, 0, 1, 1, 0, 1))
         turn = pick(i, (-1, -2, -3, -1, -2, -3), (1, 1, 3, 2, 3, 2), (1, 2, 1, 2, 3, 3))
         step = turn
         for n in range(STEPS - 1):
-            step = jnp.where(turn == -1 - n, usual_steps[n], step)
+            step = jnp.where(turn == -1 - n, usual_steps(group)[n], step)
         done = pick(i, (0, 0, 1, 0, 0, 1), (1, 1, 0, 1, 0, 1), (0, 1, 0, 1, 1, 1))
         handing = step == first_step
 
-        def arrive(piece):
-            kv_wait(step - 1, piece)
-            pl.when(handing)(lambda: hand_copy(piece).start())
+        def arrive(known):
+            for piece in (2 * known, 2 * known + 1):
+                kv_wait(step - 1, piece)
+                pl.when(handing)(lambda: hand_copy(piece).start())
 
         for known in range(groups):
             pl.when(group == known)(lambda: arrive(known))
-        pl.when(group == 0)(lambda: arrive(VALUES))
         part = met_block(step, group)
 
         @pl.when(done == 1)
@@ -351,14 +396,19 @@
     for p in range(pairs):
         x_copy(first, 0, p).wait_send()
         x_copy(second, 1, p).wait_send()
-    for piece in range(groups + 1):
+    for piece in range(2 * groups):
         kv_copy(0, 1, piece).wait_send()
         kv_copy(1, 3, piece).wait_send()
         hand_copy(piece).wait_send()
 
     @pl.when(relay)
     def _():
-        for piece in range(groups + 1):
+        for piece in range(2, 2 * groups):
+            relay_copy(piece).wait_send()
+
+    @pl.when(relay_all)
+    def _():
+        for piece in range(2):
             relay_copy(piece).wait_send()
 
 
@@ -414,10 +464,11 @@
             pltpu.VMEM((pairs, number, 2 * HEAD), bf16),
             pltpu.VMEM((number, columns), f32),
             pltpu.SemaphoreType.DMA((10,)),
-            pltpu.SemaphoreType.DMA((STEPS, groups + 1)),
-            pltpu.SemaphoreType.DMA((STEPS, groups + 1)),
+            pltpu.SemaphoreType.DMA((STEPS, 2 * groups)),
+            pltpu.SemaphoreType.DMA((STEPS, 2 * groups)),
             pltpu.SemaphoreType.DMA((2, pairs)),
             pltpu.SemaphoreType.DMA((2, pairs)),
+            pltpu.SemaphoreType.REGULAR,
         ],
         compiler_params=pltpu.CompilerParams(collective_id=0, has_side_effects=True, vmem_limit_bytes=60 << 20),
     )(queries, keys, values, positions.reshape(number // HEAD, HEAD), frequency, out_weight)
@@ -427,7 +478,7 @@
         out_shape=jax.ShapeDtypeStruct((number, columns), bf16),
         in_specs=[pl.BlockSpec(memory_space=pltpu.MemorySpace.VMEM)],
         out_specs=pl.BlockSpec(memory_space=pltpu.MemorySpace.HBM),
-        scratch_shapes=[pltpu.SemaphoreType.DMA((8,))],
+        scratch_shapes=[pltpu.SemaphoreType.DMA((4,))],
     )(pltpu.with_memory_space_constraint(projected, pltpu.MemorySpace.VMEM))
 
 

time: 38.3 us -> 37.6 us (0.982)
  Pallas kernels: 38.2 us -> 37.5 us
    pallas_call x1, Pallas kernels: 36.8 us -> 36.1 us  [shards(): pl.pallas_call(functools.partial(kernel, cycle), name='attend_and_project...]
where the time goes in v3:
time: 37.6 us; the launch traced here: 37.5 us
  Pallas kernels  37.5 us (100%)
    pallas_call x1, Pallas kernels, shards(): pl.pallas_call(functools.partial(kernel, cycle), name='attend_and_project...  36.1 us
    pallas_call x1, Pallas kernels, shards(): pl.pallas_call(store, name='store', out_shape=jax.ShapeDtypeStruct((numbe...  1.35 us

profile of v3, /device:TPU:1, one launch (start us, length us, event | category | flops | bytes accessed | tf_op | source)
XLA Modules:
  0.0 37.5 jit_solution(16383800978226275888)
XLA Ops:
  0.0 36.1 %attend_and_project.1.value_ref = bf16[512,2048]{1,0:T(8,128)(2,1)S(1)} custom-call(bf16[512,1024]{1,0:T(8,128)(2,1)} %q_hbm.1, bf16[512,256]{1,0:T(8,128)(2,1)} %k_hbm.1, bf16[512,256]{1,0:T(8,128)(2,1)} %v_hbm.1, s32[4,128]{1,0:T(4,128)} %bitcast.1, f32[8,128]{1,0:T(8,128)} %constant.2.clone.freq_hbm, bf16[2048,2048]{1,0:T(8,128)(2,1)} %w_hbm.1), custom_call_target="tpu_custom_call" | custom-call | tf_op jit(solution)/shard_map/attend_and_project/pallas_call | solution.py:439
  36.1 1.3 %store.1 = bf16[512,2048]{1,0:T(8,128)(2,1)} custom-call(bf16[512,2048]{1,0:T(8,128)(2,1)S(1)} %attend_and_project.1.value_ref), custom_call_target="tpu_custom_call" | custom-call | tf_op jit(solution)/shard_map/store/pallas_call | solution.py:475

commit v4 on v3

--- a/solution.py
+++ b/solution.py
@@ -267,7 +267,7 @@
         for m in range(per_group):
             own_block(second, group * per_group + m)
 
-        @pl.when(relay & (group == 0))
+        @pl.when((relay_all & (group == 0)) | (relay_one & (group == 1)))
         def _():
             pl.when(relay_all)(lambda: pass_on(1))
             pl.when(relay_one & jnp.logical_not(wrapped))(lambda: pl.semaphore_wait(ready, 1))

time: 37.6 us -> 37.6 us (level)
  no operation moved by 1% of the time
where the time goes in v4:
time: 37.6 us; the launch traced here: 37.5 us
  Pallas kernels  37.5 us (100%)
    pallas_call x1, Pallas kernels, shards(): pl.pallas_call(functools.partial(kernel, cycle), name='attend_and_project...  36.1 us
    pallas_call x1, Pallas kernels, shards(): pl.pallas_call(store, name='store', out_shape=jax.ShapeDtypeStruct((numbe...  1.35 us

profile of v4, /device:TPU:1, one launch (start us, length us, event | category | flops | bytes accessed | tf_op | source)
XLA Modules:
  0.0 37.5 jit_solution(15040861479380500000)
XLA Ops:
  0.0 36.1 %attend_and_project.1.value_ref = bf16[512,2048]{1,0:T(8,128)(2,1)S(1)} custom-call(bf16[512,1024]{1,0:T(8,128)(2,1)} %q_hbm.1, bf16[512,256]{1,0:T(8,128)(2,1)} %k_hbm.1, bf16[512,256]{1,0:T(8,128)(2,1)} %v_hbm.1, s32[4,128]{1,0:T(4,128)} %bitcast.1, f32[8,128]{1,0:T(8,128)} %constant.2.clone.freq_hbm, bf16[2048,2048]{1,0:T(8,128)(2,1)} %w_hbm.1), custom_call_target="tpu_custom_call" | custom-call | tf_op jit(solution)/shard_map/attend_and_project/pallas_call | solution.py:439
  36.1 1.3 %store.1 = bf16[512,2048]{1,0:T(8,128)(2,1)} custom-call(bf16[512,2048]{1,0:T(8,128)(2,1)S(1)} %attend_and_project.1.value_ref), custom_call_target="tpu_custom_call" | custom-call | tf_op jit(solution)/shard_map/store/pallas_call | solution.py:475

commit v5 on v3

--- a/solution.py
+++ b/solution.py
@@ -325,7 +325,7 @@
         return jnp.where(block == 1, listed(one), jnp.where(block == 2, listed(two), listed(usual)))
 
     def usual_steps(group):
-        late = (place < 2) & (group == 1)
+        late = (place < 2) & (group == 1) & (block >= 8)
         return (
             jnp.where(late, other_step, first_step),
             jnp.where(late, first_step, jnp.where(place == 2, 2, other_step)),

time: 37.6 us -> 36.7 us (0.976)
  Pallas kernels: 37.5 us -> 36.4 us
    pallas_call x1, Pallas kernels: 36.1 us -> 35.1 us  [shards(): pl.pallas_call(functools.partial(kernel, cycle), name='attend_and_project...]
where the time goes in v5:
time: 36.7 us; the launch traced here: 36.4 us
  Pallas kernels  36.4 us (99%)
    pallas_call x1, Pallas kernels, shards(): pl.pallas_call(functools.partial(kernel, cycle), name='attend_and_project...  35.1 us
    pallas_call x1, Pallas kernels, shards(): pl.pallas_call(store, name='store', out_shape=jax.ShapeDtypeStruct((numbe...  1.35 us

profile of v5, /device:TPU:1, one launch (start us, length us, event | category | flops | bytes accessed | tf_op | source)
XLA Modules:
  0.0 36.4 jit_solution(14577924172261424644)
XLA Ops:
  0.0 35.1 %attend_and_project.1.value_ref = bf16[512,2048]{1,0:T(8,128)(2,1)S(1)} custom-call(bf16[512,1024]{1,0:T(8,128)(2,1)} %q_hbm.1, bf16[512,256]{1,0:T(8,128)(2,1)} %k_hbm.1, bf16[512,256]{1,0:T(8,128)(2,1)} %v_hbm.1, s32[4,128]{1,0:T(4,128)} %bitcast.1, f32[8,128]{1,0:T(8,128)} %constant.2.clone.freq_hbm, bf16[2048,2048]{1,0:T(8,128)(2,1)} %w_hbm.1), custom_call_target="tpu_custom_call" | custom-call | tf_op jit(solution)/shard_map/attend_and_project/pallas_call | solution.py:439
  35.1 1.3 %store.1 = bf16[512,2048]{1,0:T(8,128)(2,1)} custom-call(bf16[512,2048]{1,0:T(8,128)(2,1)S(1)} %attend_and_project.1.value_ref), custom_call_target="tpu_custom_call" | custom-call | tf_op jit(solution)/shard_map/store/pallas_call | solution.py:475
